TPU v7x, 32 devices: a whole 2x2x4 slice. The times are simulated.
32 devices in a mesh: rows: 4 (over z), cent: 8 (over y, x, core).
Axes of the slice: x: 2, y: 2, z: 4, core: 2. Of those that a mesh axis runs over, the one named last changes fastest.
Arguments:
- train_rows: float32 [16384, 64], P('rows'), may hold values from -6 to 6
- centre_index: int32 [16384], P('cent'), may hold values from 0 to 16383
- precond: bfloat16 [16384, 16384], P('cent', 'rows'), as said below
- coefficients: float32 [16384, 128], P(('rows', 'cent')), may hold values from -6 to 6
- residual: float32 [16384, 128], P(('rows', 'cent')), may hold values from -6 to 6
- direction: float32 [16384, 128], P(('rows', 'cent')), may hold values from -6 to 6
Outputs:
- coef_next: float32 [16384, 128], P(('rows', 'cent'))
- residual_next: float32 [16384, 128], P(('rows', 'cent'))
- direction_next: float32 [16384, 128], P(('rows', 'cent'))
Inputs may be any that keep to these rules, and one draw needn't show every extreme that they name: precond is zero below its diagonal.
All inputs are finite; a program needn't handle non-finite values.
Results may differ from a plain program's by a relative error of at most 0.0047.
Values may be sent and summed in bfloat16 or wider, within the bound.
A program may use at most 128 MiB of HBM per device.

v0:
```python
import math

import jax
import jax.numpy as jnp
from jax import lax
from jax.sharding import PartitionSpec as P

FEAT = 64
OUTS = 128


ridge_weight = 0.1


def kernel_tile(block_rows, centres):
    row_sq = jnp.sum(block_rows * block_rows, axis=1)
    cen_sq = jnp.sum(centres * centres, axis=1)
    cross = jnp.dot(
        block_rows, centres.T, precision=lax.Precision.HIGHEST, preferred_element_type=jnp.float32
    )
    distance = row_sq[:, None] + cen_sq[None, :] - 2.0 * cross
    return jnp.exp(-(2.0 / FEAT) * distance).astype(jnp.bfloat16)


def kernel_pass(local_rows, centres, coef_field, combine):
    count_rows = local_rows.shape[0]
    block_size = math.gcd(count_rows, 1024)
    block_count = count_rows // block_size
    groups = local_rows.reshape(block_count, block_size, FEAT)
    tiles = lax.map(lambda group_rows: kernel_tile(group_rows, centres), groups)
    fitted_part = jnp.einsum(
        "kbc,cd->kbd", tiles, coef_field, preferred_element_type=jnp.float32
    ).reshape(count_rows, OUTS)
    fitted = combine(fitted_part)
    fitted_groups = fitted.reshape(block_count, block_size, OUTS)
    grad_part = jnp.einsum("kbc,kbd->cd", tiles, fitted_groups, preferred_element_type=jnp.float32)
    return grad_part


def on_device(train_rows, centre_index, precond, coefficients, residual, direction):
    rows_here = train_rows.shape[0]
    start_row = lax.axis_index("rows") * rows_here
    offset = centre_index - start_row
    inside = ((offset >= 0) & (offset < rows_here)).astype(jnp.float32)
    picked = train_rows[jnp.clip(offset, 0, rows_here - 1)] * inside[:, None]
    centres = lax.psum(picked, "rows")
    dir_low = direction.astype(jnp.bfloat16)
    columns = precond
    partial_field = jnp.dot(
        columns,
        lax.all_gather(dir_low, "cent", axis=0, tiled=True),
        preferred_element_type=jnp.float32,
    )
    coef_field = lax.psum(partial_field, "rows").astype(jnp.bfloat16)

    def line_sum(part):
        return lax.psum(part, "cent").astype(jnp.bfloat16)

    grad_part = kernel_pass(train_rows, centres, coef_field, line_sum)
    grad = lax.psum(grad_part, "rows")
    grad_low = (grad * float(rows_here * lax.axis_size("rows")) ** (-0.5)).astype(jnp.bfloat16)
    columns = precond
    image = lax.psum_scatter(
        lax.dot_general(
            columns, grad_low, (((0,), (0,)), ((), ())), preferred_element_type=jnp.float32
        ),
        "cent",
        scatter_dimension=0,
        tiled=True,
    )
    image = image + ridge_weight * direction
    norm_old, curvature = lax.psum(
        (jnp.sum(residual * residual), jnp.sum(direction * image)), ("rows", "cent")
    )
    step_size = norm_old / curvature
    coef_next = coefficients + step_size * direction
    residual_next = residual - step_size * image
    norm_new = lax.psum(jnp.sum(residual_next * residual_next), ("rows", "cent"))
    direction_next = residual_next + norm_new / norm_old * direction
    return (coef_next, residual_next, direction_next)


def solution(mesh):
    placed = (
        P("rows", None),
        P("cent"),
        P("cent", "rows"),
        P(("rows", "cent"), None),
        P(("rows", "cent"), None),
        P(("rows", "cent"), None),
    )
    return jax.shard_map(
        on_device,
        mesh=mesh,
        in_specs=placed,
        out_specs=(P(("rows", "cent"), None), P(("rows", "cent"), None), P(("rows", "cent"), None)),
        check_vma=False,
    )
```

profile of v0, /device:TPU:0, one launch (start us, length us, event | category | flops | bytes accessed | tf_op | source)
XLA Modules:
  0.0 441.3 jit_solution(3471181950002680406)
XLA Ops:
  8.0 0.7 fusion.8
  8.8 0.7 and_convert_fusion
  9.5 1.8 copy.9
  11.3 5.5 %gather_fusion = f32[2048,64]{1,0:T(8,128)S(1)} fusion(f32[4096,64]{1,0:T(8,128)S(1)} %copy.9, s32[2048]{0:T(1024)S(1)} %fusion.8), kind=kCustom, calls=%fused_computation | custom fusion | bytes 1056768 | tf_op jit(solution)/shard_map/gather | solution.py:45
  16.8 1.3 broadcast_multiply_fusion
  18.2 1.6 convert_element_type.21
  19.9 53.0 %all-reduce.6.cloned.1.call-done = f32[2048,64]{1,0:T(8,128)} async-done(((f32[2048,64]{1,0:T(8,128)}), f32[2048,64]{1,0:T(8,128)}) %all-reduce.6.cloned.1.call-update) | async-done | bytes 524304 | tf_op jit(solution)/shard_map/psum | solution.py:46
  72.9 1.6 multiply_reduce_fusion
  74.4 45.0 %while.12 = (s32[]{:T(128)}, bf16[4,1024,2048]{2,1,0:T(8,128)(2,1)}, f32[4,1024,64]{2,1,0:T(8,128)S(1)}, f32[2048]{0:T(1024)S(1)}, f32[2048,64]{1,0:T(8,128)}, /*index=5*/s32[]{:T(128)}) while((s32[]{:T(128)}, bf16[4,1024,2048]{2,1,0:T(8,128)(2,1)}, f32[4,1024,64]{2,1,0:T(8,128)S(1)}, f32[2048]{0:T(1024)S(1)}, f32[2048,64]{1,0:T(8,128)}, ...), condition=%wide.region_6.7_spmd, body=%wide.region_4.0_spmd.sunk | while | flops 1621228544 | bytes 6046793 | solution.py:30
  74.4 0.2 fusion.23
  74.7 11.0 %bitcast_dynamic-update-slice_fusion.2 = bf16[4,1024,2048]{2,1,0:T(8,128)(2,1)} fusion(bf16[4,1024,2048]{2,1,0:T(8,128)(2,1)} %get-tuple-element.116, s32[]{:T(128)} %get-tuple-element.115, f32[2048,64]{1,0:T(8,128)} %get-tuple-element.125, f32[2048]{0:T(1024)S(1)} %get-tuple-element.124, f32[1024]{0:T(1024)S(1)} %fusion.23, ...), kind=kOutput, calls=%fused_computation.2.clone.1 | convolution fusion | flops 1621098496 | bytes 5780480 | tf_op jit(solution)/shard_map/while/body/eval_jaxpr/dot_general | solution.py:18
  85.7 0.2 fusion.23
  85.9 11.1 %bitcast_dynamic-update-slice_fusion.2 = bf16[4,1024,2048]{2,1,0:T(8,128)(2,1)} fusion(bf16[4,1024,2048]{2,1,0:T(8,128)(2,1)} %get-tuple-element.116, s32[]{:T(128)} %get-tuple-element.115, f32[2048,64]{1,0:T(8,128)} %get-tuple-element.125, f32[2048]{0:T(1024)S(1)} %get-tuple-element.124, f32[1024]{0:T(1024)S(1)} %fusion.23, ...), kind=kOutput, calls=%fused_computation.2.clone.1 | convolution fusion | flops 1621098496 | bytes 5780480 | tf_op jit(solution)/shard_map/while/body/eval_jaxpr/dot_general | solution.py:18
  97.0 0.2 fusion.23
  97.2 11.0 %bitcast_dynamic-update-slice_fusion.2 = bf16[4,1024,2048]{2,1,0:T(8,128)(2,1)} fusion(bf16[4,1024,2048]{2,1,0:T(8,128)(2,1)} %get-tuple-element.116, s32[]{:T(128)} %get-tuple-element.115, f32[2048,64]{1,0:T(8,128)} %get-tuple-element.125, f32[2048]{0:T(1024)S(1)} %get-tuple-element.124, f32[1024]{0:T(1024)S(1)} %fusion.23, ...), kind=kOutput, calls=%fused_computation.2.clone.1 | convolution fusion | flops 1621098496 | bytes 5780480 | tf_op jit(solution)/shard_map/while/body/eval_jaxpr/dot_general | solution.py:18
  108.4 11.1 %bitcast_dynamic-update-slice_fusion.2 = bf16[4,1024,2048]{2,1,0:T(8,128)(2,1)} fusion(bf16[4,1024,2048]{2,1,0:T(8,128)(2,1)} %get-tuple-element.116, s32[]{:T(128)} %get-tuple-element.115, f32[2048,64]{1,0:T(8,128)} %get-tuple-element.125, f32[2048]{0:T(1024)S(1)} %get-tuple-element.124, f32[1024]{0:T(1024)S(1)} %fusion.23, ...), kind=kOutput, calls=%fused_computation.2.clone.1 | convolution fusion | flops 1621098496 | bytes 5780480 | tf_op jit(solution)/shard_map/while/body/eval_jaxpr/dot_general | solution.py:18
  119.5 8.4 %fusion.10 = f32[2048,128]{1,0:T(8,128)S(1)} fusion(bf16[2048,4096]{1,0:T(8,128)(2,1)} %param.10, bf16[4096,128]{1,0:T(8,128)(2,1)} %all-gather.2.cloned.1.call-done), kind=kOutput, calls=%fused_computation.28 | convolution fusion | flops 2147483648 | bytes 18874368 | tf_op jit(solution)/shard_map/dot_general | solution.py:49
  127.9 41.5 %all-reduce.9 = bf16[2048,128]{1,0:T(8,128)(2,1)S(1)} all-reduce(f32[2048,128]{1,0:T(8,128)S(1)} %fusion.10), channel_id=1, replica_groups=mesh['rows'=4,'cent'=8] {'rows'}, use_global_device_ids=true, to_apply=%region_7.8 | all-reduce | flops 262144 | bytes 1572864 | tf_op jit(solution)/shard_map/psum | solution.py:54
  169.4 8.1 %fusion.4 = f32[4,1024,128]{2,1,0:T(8,128)S(1)} fusion(bf16[4,1024,2048]{2,1,0:T(8,128)(2,1)} %get-tuple-element.58, bf16[2048,128]{1,0:T(8,128)(2,1)S(1)} %all-reduce.9), kind=kOutput, calls=%fused_computation.12 | convolution fusion | flops 2147483648 | bytes 19398656 | tf_op jit(solution)/shard_map/kbc,cd->kbd/dot_general | solution.py:31
  177.6 56.5 %all-reduce.10 = bf16[4096,128]{1,0:T(8,128)(2,1)S(1)} all-reduce(f32[4096,128]{1,0:T(8,128)S(1)} %bitcast.34), channel_id=1, replica_groups=mesh['rows'=4,'cent'=8] {'cent'}, use_global_device_ids=true, to_apply=%region_8.9 | all-reduce | flops 524288 | bytes 3145728 | tf_op jit(solution)/shard_map/psum | solution.py:57
  234.1 9.2 %convolution_bitcast_fusion.1 = f32[2048,128]{1,0:T(8,128)} fusion(bf16[4,1024,2048]{2,1,0:T(8,128)(2,1)} %get-tuple-element.58, bf16[4,1024,128]{2,1,0:T(8,128)(2,1)S(1)} %bitcast.35), kind=kOutput, calls=%fused_computation.9 | convolution fusion | flops 2147483648 | bytes 18874368 | tf_op jit(solution)/shard_map/kbc,kbd->cd/dot_general | solution.py:36
  243.3 50.7 %all-reduce.8.cloned.1.call-done = f32[2048,128]{1,0:T(8,128)} async-done(((f32[2048,128]{1,0:T(8,128)}), f32[2048,128]{1,0:T(8,128)}) %all-reduce.8.cloned.1.call-update) | async-done | bytes 1048592 | tf_op jit(solution)/shard_map/psum | solution.py:60
  294.1 9.8 %convolution_bitcast_fusion = f32[4096,128]{0,1:T(8,128)} fusion(bf16[2048,4096]{1,0:T(8,128)(2,1)} %param.10, f32[2048,128]{1,0:T(8,128)} %all-reduce.8.cloned.1.call-done), kind=kOutput, calls=%fused_computation.8 | convolution fusion | flops 2148007936 | bytes 19922944 | tf_op jit(solution)/shard_map/dot_general | solution.py:64
  304.2 0.7 multiply_reduce_fusion.3
  304.9 39.4 %reduce-scatter.2.cloned.1.call-done = f32[512,128]{0,1:T(8,128)} async-done(((f32[4096,128]{0,1:T(8,128)}), f32[512,128]{0,1:T(8,128)}) %reduce-scatter.2.cloned.1.call-update) | async-done | bytes 262160 | tf_op jit(solution)/shard_map/reduce_scatter | solution.py:63
  344.3 1.6 multiply_reduce_fusion.2
  346.0 39.6 %all-reduce = (f32[]{:T(128)}, f32[]{:T(128)}) all-reduce(f32[]{:T(128)} %multiply_reduce_fusion.3, f32[]{:T(128)} %multiply_reduce_fusion.2), channel_id=1, replica_groups=mesh['rows'=4,'cent'=8] {'rows','cent'}, use_global_device_ids=true, to_apply=%region_1.2 | all-reduce | flops 2 | bytes 16 | tf_op jit(solution)/shard_map/psum | solution.py:72
  387.0 1.6 multiply_reduce_fusion.1
  388.6 41.3 %psum.55 = f32[]{:T(128)} all-reduce(f32[]{:T(128)} %get-tuple-element.74), channel_id=1, replica_groups=mesh['rows'=4,'cent'=8] {'rows','cent'}, use_global_device_ids=true, to_apply=%region_14.15 | all-reduce | flops 1 | bytes 8 | tf_op jit(solution)/shard_map/psum | solution.py:78
  431.3 0.8 copy.18
  432.2 0.8 copy.17
  433.0 0.8 copy.19
  (21 shorter events, 0.9 us)
Async XLA Ops:
  8.0 64.9 %all-reduce.6.cloned.1.call-start = ((), (), s32[]{:S(2)}) async-start(), calls=%async_computation.1 | async-start | bytes 2097152 | tf_op jit(solution)/shard_map/psum | solution.py:46
  18.1 101.4 %all-gather.2.cloned.1.call-start = ((), (), s32[]{:S(2)}) async-start(), calls=%async_computation.2 | async-start | bytes 1179648 | tf_op jit(solution)/shard_map/all_gather | solution.py:51
  19.8 274.3 %all-reduce.8.cloned.1.call-start = ((), (), s32[]{:S(2)}) async-start(), calls=%async_computation.3 | async-start | bytes 2097152 | tf_op jit(solution)/shard_map/psum | solution.py:60
  243.3 60.6 %copy-start = (f32[512,128]{1,0:T(8,128)S(1)}, f32[512,128]{1,0:T(8,128)}, u32[]{:S(2)}) copy-start(f32[512,128]{1,0:T(8,128)} %param.13) | copy-start | bytes 786436
  243.3 60.8 %copy-start.1 = (f32[512,128]{1,0:T(8,128)S(1)}, f32[512,128]{1,0:T(8,128)}, u32[]{:S(2)}) copy-start(f32[512,128]{1,0:T(8,128)} %param.12) | copy-start | bytes 786436
  243.3 102.6 %copy-start.2 = (f32[512,128]{1,0:T(8,128)S(1)}, f32[512,128]{1,0:T(8,128)}, u32[]{:S(2)}) copy-start(f32[512,128]{1,0:T(8,128)} %param.11) | copy-start | bytes 786436
  243.3 101.0 %reduce-scatter.2.cloned.1.call-start = ((), (), s32[]{:S(2)}) async-start(), calls=%async_computation.4 | async-start | bytes 2359296 | tf_op jit(solution)/shard_map/reduce_scatter | solution.py:63
Sparse Core Ops, SparseCore 0:
  18.2 54.5 all-reduce.5
  243.4 50.5 all-reduce.7
Sparse Core Ops, SparseCore 1:
  21.1 25.9 all-gather.1
  304.0 40.2 reduce-scatter.1
where the time goes:
time: 442 us; the launch traced here: 441 us
  blocking collectives  179 us (40%)
  waiting for transfers between devices  143 us (32%)
  matrix products  79.7 us (18%)
  between operations  18.3 us (4%)
  other arithmetic  10.7 us (2%)
  local copies, waits for them, and re-layouts  10.2 us (2%)
    psum x1, blocking collectives, line_sum(): return lax.psum(part, 'cent').astype(jnp.bfloat16)  56.5 us
    psum x1, waiting for transfers between devices, on_device(): centres = lax.psum(picked, 'rows')  53 us
    psum x1, waiting for transfers between devices, on_device(): grad = lax.psum(grad_part, 'rows')  50.7 us
    dot_general x4, matrix products, kernel_tile(): jnp.dot(block_rows, centres.T, precision=lax.Precision.HIGHEST, preferred...  44.2 us
    psum x1, blocking collectives, on_device(): coef_field = lax.psum(partial_field, 'rows').astype(jnp.bfloat16)  41.5 us
    psum x1, blocking collectives, on_device(): lax.psum(jnp.sum(residual_next * residual_next), ('rows', 'cent'))  41.3 us
    psum x1, blocking collectives, on_device(): lax.psum((jnp.sum(residual * residual), jnp.sum(direction * image)), ('ro...  39.6 us
    reduce_scatter x1, waiting for transfers between devices, on_device(): lax.psum_scatter(lax.dot_general(columns, grad_low, (((0,), (0,)), ((), (...  39.4 us
  transfers between devices with their start and end apart: 4, of which 3 were waited for; matrix products, arithmetic and copies ran while one was open for 11% of the time, Pallas kernels for 0%

commit v1 on v0

v1 whole, which is shorter than its diff:
```python
import functools
import math

import jax
import jax.numpy as jnp
from jax import lax
from jax.experimental import pallas as pl
from jax.experimental.pallas import tpu as pltpu
from jax.sharding import PartitionSpec as P

FEAT = 64
OUTS = 128
CHUNK = 256
F32 = jnp.float32
BF16 = jnp.bfloat16
MESH = pl.DeviceIdType.MESH
POINT_SCALE = math.sqrt(4.0 / FEAT * math.log2(math.e))

ridge_weight = 0.1


def dot(a, b):
    return jnp.dot(a, b, preferred_element_type=F32)


def three(value):
    high = value.astype(BF16)
    rest = value - high.astype(F32)
    middle = rest.astype(BF16)
    low = (rest - middle.astype(F32)).astype(BF16)
    return high.astype(F32), middle.astype(F32), low.astype(F32)


def step_kernel(
    rows_n, cent_n,
    idx_ref, x_ref, p_hbm, res_ref, dir_ref,
    image_ref, sums_ref,
    p_buf, p_sem, k_buf, xaug, xhl_t, caug_t,
    pick, coef, grad, coef_low,
    dir_own, dir_all, fit_own, fit_all, gather_sems,
    fit_acc, fit_rs, img_acc, img_rs,
    sc_own, sc_cent, sc_mid, sc_rows, sc_sems,
):
    z = lax.axis_index("rows")
    me = lax.axis_index("cent")
    core = lax.rem(me, 2)
    chip = lax.div(me, 2)
    other = chip * 2 + (1 - core)
    chips = cent_n // 2
    chunks = p_buf.shape[0]
    rows_here = x_ref.shape[0]
    part = dir_own.shape[0]
    fit_part = fit_acc.shape[1]
    last = rows_n - 1

    def chip_at(distance):
        return lax.rem(chip + distance, chips)

    def p_copy(k):
        return pltpu.make_async_copy(
            p_hbm.at[pl.ds(pl.multiple_of(k * CHUNK, CHUNK), CHUNK)], p_buf.at[k], p_sem.at[k]
        )

    @pl.loop(0, chunks)
    def _(k):
        p_copy(k).start()

    barrier = pltpu.get_barrier_semaphore()
    for d in range(1, cent_n):
        pl.semaphore_signal(
            barrier, inc=1, device_id=(z, lax.rem(me + d, cent_n)), device_id_type=MESH
        )
    for d in range(1, rows_n):
        pl.semaphore_signal(
            barrier, inc=1, device_id=(lax.rem(z + d, rows_n), me), device_id_type=MESH
        )
    dir_own[...] = dir_ref[...].astype(BF16)
    pl.semaphore_wait(barrier, cent_n - 1 + rows_n - 1)

    def gather_copy(which, own, whole, d):
        target = other if d == 0 else chip_at(d) * 2 + core
        return pltpu.make_async_remote_copy(
            src_ref=own, dst_ref=whole.at[me],
            send_sem=gather_sems.at[which, 0, d], recv_sem=gather_sems.at[which, 1, d],
            device_id=(z, target), device_id_type=MESH,
        )

    def forward_copy(which, whole, d):
        source = chip_at(chips - d) * 2 + core
        return pltpu.make_async_remote_copy(
            src_ref=whole.at[source], dst_ref=whole.at[source],
            send_sem=gather_sems.at[which, 2, d], recv_sem=gather_sems.at[which, 3, d],
            device_id=(z, other), device_id_type=MESH,
        )

    def gather_start(which, own, whole):
        for d in list(range(1, chips)) + [0]:
            gather_copy(which, own, whole, d).start()
        whole[me] = own[...]

    def gather_forward(which, own, whole):
        for d in range(1, chips):
            gather_copy(which, own, whole, d).wait_recv()
            forward_copy(which, whole, d).start()

    def gather_end(which, own, whole):
        gather_copy(which, own, whole, 0).wait_recv()
        for d in range(1, chips):
            forward_copy(which, whole, d).wait_recv()
        for d in range(chips):
            gather_copy(which, own, whole, d).wait_send()
        for d in range(1, chips):
            forward_copy(which, whole, d).wait_send()

    def right_copy(scan, k):
        own, to_right, to_left, from_left, from_right, sems = scan
        return pltpu.make_async_remote_copy(
            src_ref=to_right.at[k], dst_ref=from_left.at[k],
            send_sem=sems.at[0, k], recv_sem=sems.at[1, k],
            device_id=(lax.rem(z + 1, rows_n), me), device_id_type=MESH,
        )

    def left_copy(scan, k):
        own, to_right, to_left, from_left, from_right, sems = scan
        return pltpu.make_async_remote_copy(
            src_ref=to_left.at[k], dst_ref=from_right.at[k],
            send_sem=sems.at[2, k], recv_sem=sems.at[3, k],
            device_id=(lax.rem(z + last, rows_n), me), device_id_type=MESH,
        )

    def scan_step(scan, it):
        own, to_right, to_left, from_left, from_right, sems = scan
        kr = it - z
        kl = it - (last - z)

        @pl.when((kr >= 0) & (kr < chunks) & (z < last))
        def _():
            @pl.when(z == 0)
            def _():
                to_right[kr] = own[kr].astype(BF16)

            @pl.when(z > 0)
            def _():
                right_copy(scan, kr).wait_recv()
                to_right[kr] = (own[kr].astype(F32) + from_left[kr].astype(F32)).astype(BF16)

            right_copy(scan, kr).start()

        @pl.when((kl >= 0) & (kl < chunks) & (z > 0))
        def _():
            @pl.when(z == last)
            def _():
                to_left[kl] = own[kl].astype(BF16)

            @pl.when(z < last)
            def _():
                left_copy(scan, kl).wait_recv()
                to_left[kl] = (own[kl].astype(F32) + from_right[kl].astype(F32)).astype(BF16)

            left_copy(scan, kl).start()

    def scan_total(scan, k):
        own, to_right, to_left, from_left, from_right, sems = scan

        @pl.when(z == last)
        def _():
            right_copy(scan, k).wait_recv()

        @pl.when(z == 0)
        def _():
            left_copy(scan, k).wait_recv()

        @pl.when(z > 0)
        def _():
            own[k] = (own[k].astype(F32) + from_left[k].astype(F32)).astype(own.dtype)

        @pl.when(z < last)
        def _():
            own[k] = (own[k].astype(F32) + from_right[k].astype(F32)).astype(own.dtype)

    def scan_sent(scan):
        @pl.loop(0, chunks)
        def _(k):
            @pl.when(z < last)
            def _():
                right_copy(scan, k).wait_send()

            @pl.when(z > 0)
            def _():
                left_copy(scan, k).wait_send()

    def across_copy(buffers, q):
        send_a, recv_a, send_b, recv_b, sems = buffers
        return pltpu.make_async_remote_copy(
            src_ref=send_a.at[q], dst_ref=recv_a.at[q],
            send_sem=sems.at[0, q], recv_sem=sems.at[1, q],
            device_id=(z, other), device_id_type=MESH,
        )

    def between_copy(buffers, d):
        send_a, recv_a, send_b, recv_b, sems = buffers
        return pltpu.make_async_remote_copy(
            src_ref=send_b.at[d], dst_ref=recv_b.at[d],
            send_sem=sems.at[2, d], recv_sem=sems.at[3, d],
            device_id=(z, chip_at(d) * 2 + core), device_id_type=MESH,
        )

    def scatter_sum(acc, buffers):
        send_a, recv_a, send_b, recv_b, sems = buffers
        for d in list(range(1, chips)) + [0]:
            q = chip_at(d)
            send_a[q] = acc[q * 2 + (1 - core)].astype(BF16)
            across_copy(buffers, q).start()
        for d in range(1, chips):
            q = chip_at(d)
            across_copy(buffers, q).wait_recv()
            send_b[d] = (acc[q * 2 + core] + recv_a[q].astype(F32)).astype(BF16)
            between_copy(buffers, d).start()
        across_copy(buffers, chip).wait_recv()
        total = acc[me] + recv_a[chip].astype(F32)
        for d in range(1, chips):
            between_copy(buffers, d).wait_recv()
            total = total + recv_b[d].astype(F32)
        for d in range(chips):
            across_copy(buffers, chip_at(d)).wait_send()
        for d in range(1, chips):
            between_copy(buffers, d).wait_send()
        return total

    gather_start(0, dir_own, dir_all)

    point_block = math.gcd(rows_here, 512)

    @pl.loop(0, rows_here // point_block)
    def _(b):
        here = pl.ds(pl.multiple_of(b * point_block, point_block), point_block)
        points = x_ref[here, :] * POINT_SCALE
        high = points.astype(BF16)
        low = (points - high.astype(F32)).astype(BF16)
        exact = high.astype(F32) + low.astype(F32)
        half = -0.5 * jnp.sum(exact * exact, axis=1, keepdims=True)
        first, second, third = three(half)
        lane = lax.broadcasted_iota(jnp.int32, (point_block, FEAT), 1)
        extra = jnp.where(
            lane == 0, first,
            jnp.where(lane == 1, second, jnp.where(lane == 2, third, jnp.where(lane < 6, 1.0, 0.0))),
        )
        high32 = high.astype(F32)
        low32 = low.astype(F32)
        xaug[here, :] = jnp.concatenate([high32, low32, high32, extra], axis=1).astype(BF16)
        xhl_t[:, here] = jnp.concatenate([high32, low32], axis=1).T.astype(BF16)

    pick_block = math.gcd(rows_here, 1024)

    @pl.loop(0, chunks + rows_n - 1)
    def _(it):
        @pl.when(it < chunks)
        def _():
            wanted = idx_ref[it] - z * rows_here
            total = jnp.zeros((2 * FEAT, CHUNK), F32)
            for b in range(rows_here // pick_block):
                ids = lax.broadcasted_iota(jnp.int32, (pick_block, CHUNK), 0) + b * pick_block
                hot = jnp.where(ids == wanted, 1.0, 0.0).astype(BF16)
                total = total + dot(xhl_t[:, b * pick_block : (b + 1) * pick_block], hot)
            pick[0][it] = total.astype(BF16)

        scan_step(pick, it)

    gather_forward(0, dir_own, dir_all)
    gather_end(0, dir_own, dir_all)

    fit_acc[...] = jnp.zeros_like(fit_acc)
    k_block = math.gcd(rows_here, 512)

    @pl.loop(0, chunks + rows_n - 1)
    def _(it):
        @pl.when(it < chunks)
        def _():
            p_copy(it).wait()
            directions = dir_all[...].reshape(cent_n * part, OUTS)
            coef[0][it] = dot(p_buf[it], directions)

        scan_step(coef, it)

        @pl.when(it < chunks)
        def _():
            scan_total(pick, it)
            pair = pick[0][it].astype(F32)
            high = pair[:FEAT]
            low = pair[FEAT:]
            exact = high + low
            half = -0.5 * jnp.sum(exact * exact, axis=0, keepdims=True)
            first, second, third = three(half)
            sub = lax.broadcasted_iota(jnp.int32, (FEAT, CHUNK), 0)
            extra = jnp.where(
                sub < 3, 1.0,
                jnp.where(sub == 3, first, jnp.where(sub == 4, second, jnp.where(sub == 5, third, 0.0))),
            )
            caug_t[...] = jnp.concatenate([high, high, low, extra], axis=0).astype(BF16)

            @pl.loop(0, rows_here // k_block)
            def _(b):
                here = pl.ds(pl.multiple_of(b * k_block, k_block), k_block)
                k_buf[it, here, :] = jnp.exp2(dot(xaug[here, :], caug_t[...])).astype(BF16)

        @pl.when(it >= rows_n - 1)
        def _():
            k = it - (rows_n - 1)
            scan_total(coef, k)
            coef_low[...] = coef[0][k].astype(BF16)

            @pl.loop(0, cent_n)
            def _(b):
                here = pl.ds(pl.multiple_of(b * fit_part, fit_part), fit_part)
                fit_acc[b] += dot(k_buf[k, here, :], coef_low[...])

    fitted = scatter_sum(fit_acc, fit_rs)
    fit_own[...] = fitted.T.astype(BF16)
    gather_start(1, fit_own, fit_all)
    img_acc[...] = jnp.zeros_like(img_acc)
    gather_forward(1, fit_own, fit_all)
    gather_end(1, fit_own, fit_all)

    scale = float(rows_here * rows_n) ** -0.5

    @pl.loop(0, chunks + rows_n - 1)
    def _(it):
        @pl.when(it < chunks)
        def _():
            total = jnp.zeros((OUTS, CHUNK), F32)
            for b in range(cent_n):
                total = total + dot(
                    fit_all[b], k_buf[it, b * fit_part : (b + 1) * fit_part, :]
                )
            grad[0][it] = total

        scan_step(grad, it)

        @pl.when(it >= rows_n - 1)
        def _():
            k = it - (rows_n - 1)
            scan_total(grad, k)
            low = (grad[0][k] * scale).astype(BF16)
            for b in range(cent_n):
                img_acc[b] += dot(low, p_buf[k, :, b * part : (b + 1) * part])

    image = scatter_sum(img_acc, img_rs).T + ridge_weight * dir_ref[...]
    image_ref[...] = image

    def rows_sum(value):
        return jnp.sum(value, axis=0, keepdims=True)

    residual = res_ref[...]
    sc_own[...] = jnp.concatenate(
        [
            rows_sum(residual * residual),
            rows_sum(dir_ref[...] * image),
            rows_sum(residual * image),
            rows_sum(image * image),
            jnp.zeros((4, OUTS), F32),
        ],
        axis=0,
    )

    def cent_copy(d):
        return pltpu.make_async_remote_copy(
            src_ref=sc_own, dst_ref=sc_cent.at[d],
            send_sem=sc_sems.at[0, d], recv_sem=sc_sems.at[1, d],
            device_id=(z, lax.rem(me + d, cent_n)), device_id_type=MESH,
        )

    def rows_copy(d):
        return pltpu.make_async_remote_copy(
            src_ref=sc_mid, dst_ref=sc_rows.at[d],
            send_sem=sc_sems.at[2, d], recv_sem=sc_sems.at[3, d],
            device_id=(lax.rem(z + d, rows_n), me), device_id_type=MESH,
        )

    for d in range(1, cent_n):
        cent_copy(d).start()
    total = sc_own[...]
    for d in range(1, cent_n):
        cent_copy(d).wait_recv()
        total = total + sc_cent[d]
    sc_mid[...] = total
    for d in range(1, rows_n):
        rows_copy(d).start()
    for d in range(1, rows_n):
        rows_copy(d).wait_recv()
        total = total + sc_rows[d]
    sums_ref[...] = total

    for d in range(1, cent_n):
        cent_copy(d).wait_send()
    for d in range(1, rows_n):
        rows_copy(d).wait_send()
    scan_sent(pick)
    scan_sent(coef)
    scan_sent(grad)


def on_device(rows_n, cent_n, train_rows, centre_index, precond, coefficients, residual, direction):
    rows_here = train_rows.shape[0]
    centres_here = centre_index.shape[0]
    part = direction.shape[0]
    chunks = centres_here // CHUNK
    chips = cent_n // 2
    fit_part = rows_here // cent_n
    vmem = pl.BlockSpec(memory_space=pltpu.VMEM)

    def scan(shape, own_dtype):
        piece = (chunks,) + shape
        return (
            pltpu.VMEM(piece, own_dtype),
            pltpu.VMEM(piece, BF16), pltpu.VMEM(piece, BF16),
            pltpu.VMEM(piece, BF16), pltpu.VMEM(piece, BF16),
            pltpu.SemaphoreType.DMA((4, chunks)),
        )

    def scatter(shape):
        piece = (chips,) + shape
        return (
            pltpu.VMEM(piece, BF16), pltpu.VMEM(piece, BF16),
            pltpu.VMEM(piece, BF16), pltpu.VMEM(piece, BF16),
            pltpu.SemaphoreType.DMA((4, chips)),
        )

    image, sums = pl.pallas_call(
        functools.partial(step_kernel, rows_n, cent_n),
        out_shape=(
            jax.ShapeDtypeStruct((part, OUTS), F32),
            jax.ShapeDtypeStruct((8, OUTS), F32),
        ),
        in_specs=[vmem, vmem, pl.BlockSpec(memory_space=pl.ANY), vmem, vmem],
        out_specs=(vmem, vmem),
        scratch_shapes=[
            pltpu.VMEM((chunks, CHUNK, precond.shape[1]), BF16),
            pltpu.SemaphoreType.DMA((chunks,)),
            pltpu.VMEM((chunks, rows_here, CHUNK), BF16),
            pltpu.VMEM((rows_here, 4 * FEAT), BF16),
            pltpu.VMEM((2 * FEAT, rows_here), BF16),
            pltpu.VMEM((4 * FEAT, CHUNK), BF16),
            scan((2 * FEAT, CHUNK), BF16),
            scan((CHUNK, OUTS), F32),
            scan((OUTS, CHUNK), F32),
            pltpu.VMEM((CHUNK, OUTS), BF16),
            pltpu.VMEM((part, OUTS), BF16),
            pltpu.VMEM((cent_n, part, OUTS), BF16),
            pltpu.VMEM((OUTS, fit_part), BF16),
            pltpu.VMEM((cent_n, OUTS, fit_part), BF16),
            pltpu.SemaphoreType.DMA((2, 4, chips)),
            pltpu.VMEM((cent_n, fit_part, OUTS), F32),
            scatter((fit_part, OUTS)),
            pltpu.VMEM((cent_n, OUTS, part), F32),
            scatter((OUTS, part)),
            pltpu.VMEM((8, OUTS), F32),
            pltpu.VMEM((cent_n, 8, OUTS), F32),
            pltpu.VMEM((8, OUTS), F32),
            pltpu.VMEM((rows_n, 8, OUTS), F32),
            pltpu.SemaphoreType.DMA((4, max(cent_n, rows_n))),
        ],
        compiler_params=pltpu.CompilerParams(
            collective_id=0, has_side_effects=True, vmem_limit_bytes=67000000
        ),
        name="falkon_step",
    )(centre_index.reshape(chunks, 1, CHUNK), train_rows, precond, residual, direction)

    totals = jnp.sum(sums, axis=1)
    norm_old, curvature, cross, square = totals[0], totals[1], totals[2], totals[3]
    step_size = norm_old / curvature
    norm_new = norm_old - 2.0 * step_size * cross + step_size * step_size * square
    coef_next = coefficients + step_size * direction
    residual_next = residual - step_size * image
    direction_next = residual_next + norm_new / norm_old * direction
    return (coef_next, residual_next, direction_next)


def solution(mesh):
    both = P(("rows", "cent"), None)
    return jax.shard_map(
        functools.partial(on_device, mesh.shape["rows"], mesh.shape["cent"]),
        mesh=mesh,
        in_specs=(P("rows", None), P("cent"), P("cent", "rows"), both, both, both),
        out_specs=(both, both, both),
        check_vma=False,
    )
```

time: 442 us -> 155 us (0.35)
  blocking collectives: 179 us -> 0 us
  Pallas kernels: 0 us -> 144 us
  waiting for transfers between devices: 143 us -> 0 us
  matrix products: 79.7 us -> 0 us
  between operations: 18.3 us -> 4.34 us
  other arithmetic: 10.7 us -> 2.9 us
  local copies, waits for them, and re-layouts: 10.2 us -> 3.78 us
    psum x4 -> x0, blocking collectives: 179 us -> none  [the longest x1 56.5 us: line_sum(): return lax.psum(part, 'cent').astype(jnp.bfloat16)]
    pallas_call x0 -> x1, Pallas kernels: none -> 144 us  [on_device(): pl.pallas_call(functools.partial(step_kernel, rows_n, cent_n), out_shape=...]
    psum x2 -> x0, waiting for transfers between devices: 104 us -> none  [the longest x1 53 us: on_device(): centres = lax.psum(picked, 'rows')]
    dot_general x8 -> x0, matrix products: 79.7 us -> none  [the longest x4 44.2 us: kernel_tile(): jnp.dot(block_rows, centres.T, precision=lax.Precision.HIGHEST, preferred...]
    reduce_scatter x1 -> x0, waiting for transfers between devices: 39.4 us -> none  [on_device(): lax.psum_scatter(lax.dot_general(columns, grad_low, (((0,), (0,)), ((), (...]
    reduce_sum x8 -> x1, other arithmetic: 6.32 us -> 0.79 us  [on_device(): totals = jnp.sum(sums, axis=1)]
    gather x1 -> x0, local copies, waits for them, and re-layouts: 5.47 us -> none  [on_device(): picked = train_rows[jnp.clip(offset, 0, rows_here - 1)] * inside[:, None]]
  transfers between devices with their start and end apart: 4 -> 0, of which waited for: 3 -> 0; matrix products, arithmetic and copies ran while one was open for 11% -> 0% of each run, Pallas kernels for 0% -> 0%
where the time goes in v1:
time: 155 us
  Pallas kernels  144 us (93%)
  between operations  4.34 us (3%)
  local copies, waits for them, and re-layouts  3.78 us (2%)
  other arithmetic  2.9 us (2%)
    pallas_call x1, Pallas kernels, on_device(): pl.pallas_call(functools.partial(step_kernel, rows_n, cent_n), out_shape=...  144 us
    unnamed x1, local copies, waits for them, and re-layouts  3.18 us

profile of v1, /device:TPU:0, one launch (start us, length us, event | category | flops | bytes accessed | tf_op | source)
XLA Modules:
  0.0 154.6 jit_solution(9222795823954902917)
XLA Ops:
  0.6 3.2 %copy.9.x_ref = f32[4096,64]{1,0:T(8,128)} copy(f32[4096,64]{0,1:T(8,128)} %param.6) | data formatting | bytes 2097152 | tf_op args[0]
  3.8 143.6 %falkon_step.1 = (f32[512,128]{1,0:T(8,128)}, f32[8,128]{1,0:T(8,128)}) custom-call(s32[8,1,256]{2,1,0:T(1,128)} %bitcast.5, f32[4096,64]{1,0:T(8,128)} %copy.9.x_ref, bf16[2048,4096]{1,0:T(8,128)(2,1)} %p_hbm.1, f32[512,128]{1,0:T(8,128)} %res_ref.1, f32[512,128]{1,0:T(8,128)} %dir_ref.1), custom_call_target="tpu_custom_call" | custom-call | tf_op jit(solution)/shard_map/falkon_step/pallas_call | solution.py:428
  147.4 0.8 reduce_sum.9
  148.2 0.6 fusion
  152.5 2.1 %multiply_add_fusion = (f32[512,128]{1,0:T(8,128)}, f32[512,128]{1,0:T(8,128)}, f32[512,128]{1,0:T(8,128)}) fusion(f32[512,128]{1,0:T(8,128)} %dir_ref.1, f32[]{:T(128)S(6)} %div.7, f32[512,128]{1,0:T(8,128)} %res_ref.1, f32[512,128]{1,0:T(8,128)} %get-tuple-element.6, f32[]{:T(128)S(6)} %div.6, f32[512,128]{1,0:T(8,128)} %param.9), kind=kLoop, calls=%fused_computation | loop fusion | flops 393216 | bytes 1835016 | tf_op jit(solution)/shard_map/add | solution.py:474

commit v2 on v1

--- a/solution.py
+++ b/solution.py
@@ -11,10 +11,11 @@
 FEAT = 64
 OUTS = 128
 CHUNK = 256
+LAG = 2
 F32 = jnp.float32
 BF16 = jnp.bfloat16
 MESH = pl.DeviceIdType.MESH
-POINT_SCALE = math.sqrt(4.0 / FEAT * math.log2(math.e))
+POINT_SCALE = math.sqrt(4.0 / FEAT)
 
 ridge_weight = 0.1
 
@@ -48,7 +49,7 @@
     other = chip * 2 + (1 - core)
     chips = cent_n // 2
     chunks = p_buf.shape[0]
-    rows_here = x_ref.shape[0]
+    rows_here = x_ref.shape[1]
     part = dir_own.shape[0]
     fit_part = fit_acc.shape[1]
     last = rows_n - 1
@@ -130,8 +131,8 @@
 
     def scan_step(scan, it):
         own, to_right, to_left, from_left, from_right, sems = scan
-        kr = it - z
-        kl = it - (last - z)
+        kr = it - LAG * z
+        kl = it - LAG * (last - z)
 
         @pl.when((kr >= 0) & (kr < chunks) & (z < last))
         def _():
@@ -229,42 +230,44 @@
 
     gather_start(0, dir_own, dir_all)
 
-    point_block = math.gcd(rows_here, 512)
-
-    @pl.loop(0, rows_here // point_block)
-    def _(b):
+    point_block = rows_here // chunks
+
+    for b in range(chunks):
+        here = slice(b * point_block, (b + 1) * point_block)
+        points = x_ref[:, here] * POINT_SCALE
+        high = points.astype(BF16)
+        xhl_t[:FEAT, here] = high
+        xhl_t[FEAT:, here] = (points - high.astype(F32)).astype(BF16)
+
+    def augmented(pair, norm_at, one_at):
+        high = pair[:FEAT]
+        low = pair[FEAT:]
+        exact = high + low
+        half = -0.5 * jnp.sum(exact * exact, axis=0, keepdims=True)
+        sub = lax.broadcasted_iota(jnp.int32, high.shape, 0)
+        extra = jnp.where((sub >= one_at) & (sub < one_at + 3), 1.0, 0.0)
+        for at, term in enumerate(three(half)):
+            extra = jnp.where(sub == norm_at + at, term, extra)
+        return high, low, extra
+
+    def augment(b):
         here = pl.ds(pl.multiple_of(b * point_block, point_block), point_block)
-        points = x_ref[here, :] * POINT_SCALE
-        high = points.astype(BF16)
-        low = (points - high.astype(F32)).astype(BF16)
-        exact = high.astype(F32) + low.astype(F32)
-        half = -0.5 * jnp.sum(exact * exact, axis=1, keepdims=True)
-        first, second, third = three(half)
-        lane = lax.broadcasted_iota(jnp.int32, (point_block, FEAT), 1)
-        extra = jnp.where(
-            lane == 0, first,
-            jnp.where(lane == 1, second, jnp.where(lane == 2, third, jnp.where(lane < 6, 1.0, 0.0))),
-        )
-        high32 = high.astype(F32)
-        low32 = low.astype(F32)
-        xaug[here, :] = jnp.concatenate([high32, low32, high32, extra], axis=1).astype(BF16)
-        xhl_t[:, here] = jnp.concatenate([high32, low32], axis=1).T.astype(BF16)
+        high, low, extra = augmented(xhl_t[:, here].astype(F32), 0, 3)
+        xaug[here, :] = jnp.concatenate([high, low, high, extra], axis=0).T.astype(BF16)
 
     pick_block = math.gcd(rows_here, 1024)
 
-    @pl.loop(0, chunks + rows_n - 1)
+    @pl.loop(0, chunks)
     def _(it):
-        @pl.when(it < chunks)
-        def _():
-            wanted = idx_ref[it] - z * rows_here
-            total = jnp.zeros((2 * FEAT, CHUNK), F32)
-            for b in range(rows_here // pick_block):
-                ids = lax.broadcasted_iota(jnp.int32, (pick_block, CHUNK), 0) + b * pick_block
-                hot = jnp.where(ids == wanted, 1.0, 0.0).astype(BF16)
-                total = total + dot(xhl_t[:, b * pick_block : (b + 1) * pick_block], hot)
-            pick[0][it] = total.astype(BF16)
-
+        wanted = idx_ref[it] - z * rows_here
+        total = jnp.zeros((2 * FEAT, CHUNK), F32)
+        for b in range(rows_here // pick_block):
+            ids = lax.broadcasted_iota(jnp.int32, (pick_block, CHUNK), 0) + b * pick_block
+            hot = jnp.where(ids == wanted, 1.0, 0.0).astype(BF16)
+            total = total + dot(xhl_t[:, b * pick_block : (b + 1) * pick_block], hot)
+        pick[0][it] = total.astype(BF16)
         scan_step(pick, it)
+        augment(it)
 
     gather_forward(0, dir_own, dir_all)
     gather_end(0, dir_own, dir_all)
@@ -272,8 +275,10 @@
     fit_acc[...] = jnp.zeros_like(fit_acc)
     k_block = math.gcd(rows_here, 512)
 
-    @pl.loop(0, chunks + rows_n - 1)
+    @pl.loop(0, chunks + LAG * last)
     def _(it):
+        scan_step(pick, it + chunks)
+
         @pl.when(it < chunks)
         def _():
             p_copy(it).wait()
@@ -285,33 +290,21 @@
         @pl.when(it < chunks)
         def _():
             scan_total(pick, it)
-            pair = pick[0][it].astype(F32)
-            high = pair[:FEAT]
-            low = pair[FEAT:]
-            exact = high + low
-            half = -0.5 * jnp.sum(exact * exact, axis=0, keepdims=True)
-            first, second, third = three(half)
-            sub = lax.broadcasted_iota(jnp.int32, (FEAT, CHUNK), 0)
-            extra = jnp.where(
-                sub < 3, 1.0,
-                jnp.where(sub == 3, first, jnp.where(sub == 4, second, jnp.where(sub == 5, third, 0.0))),
-            )
+            high, low, extra = augmented(pick[0][it].astype(F32), 3, 0)
             caug_t[...] = jnp.concatenate([high, high, low, extra], axis=0).astype(BF16)
 
-            @pl.loop(0, rows_here // k_block)
-            def _(b):
-                here = pl.ds(pl.multiple_of(b * k_block, k_block), k_block)
-                k_buf[it, here, :] = jnp.exp2(dot(xaug[here, :], caug_t[...])).astype(BF16)
-
-        @pl.when(it >= rows_n - 1)
-        def _():
-            k = it - (rows_n - 1)
+            for b in range(rows_here // k_block):
+                here = slice(b * k_block, (b + 1) * k_block)
+                k_buf[it, here, :] = jnp.exp(dot(xaug[here, :], caug_t[...])).astype(BF16)
+
+        @pl.when(it >= LAG * last)
+        def _():
+            k = it - LAG * last
             scan_total(coef, k)
             coef_low[...] = coef[0][k].astype(BF16)
 
-            @pl.loop(0, cent_n)
-            def _(b):
-                here = pl.ds(pl.multiple_of(b * fit_part, fit_part), fit_part)
+            for b in range(cent_n):
+                here = slice(b * fit_part, (b + 1) * fit_part)
                 fit_acc[b] += dot(k_buf[k, here, :], coef_low[...])
 
     fitted = scatter_sum(fit_acc, fit_rs)
@@ -323,7 +316,7 @@
 
     scale = float(rows_here * rows_n) ** -0.5
 
-    @pl.loop(0, chunks + rows_n - 1)
+    @pl.loop(0, chunks + LAG * last)
     def _(it):
         @pl.when(it < chunks)
         def _():
@@ -336,9 +329,9 @@
 
         scan_step(grad, it)
 
-        @pl.when(it >= rows_n - 1)
-        def _():
-            k = it - (rows_n - 1)
+        @pl.when(it >= LAG * last)
+        def _():
+            k = it - LAG * last
             scan_total(grad, k)
             low = (grad[0][k] * scale).astype(BF16)
             for b in range(cent_n):
@@ -397,6 +390,19 @@
     scan_sent(pick)
     scan_sent(coef)
     scan_sent(grad)
+
+
+def update_kernel(sums_ref, image_ref, coef_ref, res_ref, dir_ref, coef_out, res_out, dir_out):
+    totals = jnp.sum(sums_ref[...], axis=1, keepdims=True)
+    norm_old, curvature, cross, square = (totals[at : at + 1] for at in range(4))
+    step_size = norm_old / curvature
+    norm_new = norm_old - 2.0 * step_size * cross + step_size * step_size * square
+    ratio = norm_new / norm_old
+    direction = dir_ref[...]
+    coef_out[...] = coef_ref[...] + step_size * direction
+    residual_next = res_ref[...] - step_size * image_ref[...]
+    res_out[...] = residual_next
+    dir_out[...] = residual_next + ratio * direction
 
 
 def on_device(rows_n, cent_n, train_rows, centre_index, precond, coefficients, residual, direction):
@@ -463,16 +469,16 @@
             collective_id=0, has_side_effects=True, vmem_limit_bytes=67000000
         ),
         name="falkon_step",
-    )(centre_index.reshape(chunks, 1, CHUNK), train_rows, precond, residual, direction)
-
-    totals = jnp.sum(sums, axis=1)
-    norm_old, curvature, cross, square = totals[0], totals[1], totals[2], totals[3]
-    step_size = norm_old / curvature
-    norm_new = norm_old - 2.0 * step_size * cross + step_size * step_size * square
-    coef_next = coefficients + step_size * direction
-    residual_next = residual - step_size * image
-    direction_next = residual_next + norm_new / norm_old * direction
-    return (coef_next, residual_next, direction_next)
+    )(centre_index.reshape(chunks, 1, CHUNK), train_rows.T, precond, residual, direction)
+
+    piece = jax.ShapeDtypeStruct((part, OUTS), F32)
+    return pl.pallas_call(
+        update_kernel,
+        out_shape=(piece, piece, piece),
+        in_specs=[vmem] * 5,
+        out_specs=(vmem, vmem, vmem),
+        name="falkon_update",
+    )(sums, image, coefficients, residual, direction)
 
 
 def solution(mesh):

time: 155 us -> 106 us (0.68)
  Pallas kernels: 144 us -> 106 us
  local copies, waits for them, and re-layouts: 3.78 us -> 0 us
  between operations: 4.34 us -> 0.64 us
  other arithmetic: 2.9 us -> 0 us
    pallas_call x1, Pallas kernels: 144 us -> 103 us  [on_device(): pl.pallas_call(functools.partial(step_kernel, rows_n, cent_n), out_shape=...]
    unnamed x1 -> x0, local copies, waits for them, and re-layouts: 3.18 us -> none
    pallas_call x0 -> x1, Pallas kernels: none -> 2.22 us  [on_device(): pl.pallas_call(update_kernel, out_shape=(piece, piece, piece), in_specs=[...]
    add x1 -> x0, other arithmetic: 2.11 us -> none  [on_device(): direction_next = residual_next + norm_new / norm_old * direction]
where the time goes in v2:
time: 106 us
  Pallas kernels  106 us (100%)
    pallas_call x1, Pallas kernels, on_device(): pl.pallas_call(functools.partial(step_kernel, rows_n, cent_n), out_shape=...  103 us
    pallas_call x1, Pallas kernels, on_device(): pl.pallas_call(update_kernel, out_shape=(piece, piece, piece), in_specs=[...  2.22 us

profile of v2, /device:TPU:0, one launch (start us, length us, event | category | flops | bytes accessed | tf_op | source)
XLA Modules:
  0.0 106.3 jit_solution(2145954222423737474)
XLA Ops:
  0.6 103.4 %falkon_step.1 = (f32[512,128]{1,0:T(8,128)}, f32[8,128]{1,0:T(8,128)}) custom-call(s32[8,1,256]{2,1,0:T(1,128)} %bitcast.3, f32[64,4096]{1,0:T(8,128)} %bitcast.2, bf16[2048,4096]{1,0:T(8,128)(2,1)} %p_hbm.1, f32[512,128]{1,0:T(8,128)} %res_ref.3, f32[512,128]{1,0:T(8,128)} %dir_ref.3), custom_call_target="tpu_custom_call" | custom-call | tf_op jit(solution)/shard_map/falkon_step/pallas_call | solution.py:434
  104.1 2.2 %falkon_update.1 = (f32[512,128]{1,0:T(8,128)}, f32[512,128]{1,0:T(8,128)}, f32[512,128]{1,0:T(8,128)}) custom-call(f32[8,128]{1,0:T(8,128)} %get-tuple-element.5.sums_ref, f32[512,128]{1,0:T(8,128)} %get-tuple-element.6.image_ref, f32[512,128]{1,0:T(8,128)} %coef_ref.1, f32[512,128]{1,0:T(8,128)} %res_ref.3, f32[512,128]{1,0:T(8,128)} %dir_ref.3), custom_call_target="tpu_custom_call" | custom-call | tf_op jit(solution)/shard_map/falkon_update/pallas_call | solution.py:475

commit v3 on v2

--- a/solution.py
+++ b/solution.py
@@ -11,7 +11,7 @@
 FEAT = 64
 OUTS = 128
 CHUNK = 256
-LAG = 2
+LAG = 3
 F32 = jnp.float32
 BF16 = jnp.bfloat16
 MESH = pl.DeviceIdType.MESH
@@ -190,43 +190,51 @@
             def _():
                 left_copy(scan, k).wait_send()
 
-    def across_copy(buffers, q):
+    def across_copy(buffers, h, q):
         send_a, recv_a, send_b, recv_b, sems = buffers
         return pltpu.make_async_remote_copy(
-            src_ref=send_a.at[q], dst_ref=recv_a.at[q],
-            send_sem=sems.at[0, q], recv_sem=sems.at[1, q],
+            src_ref=send_a.at[h, q], dst_ref=recv_a.at[h, q],
+            send_sem=sems.at[h, 0, q], recv_sem=sems.at[h, 1, q],
             device_id=(z, other), device_id_type=MESH,
         )
 
-    def between_copy(buffers, d):
+    def between_copy(buffers, h, d):
         send_a, recv_a, send_b, recv_b, sems = buffers
         return pltpu.make_async_remote_copy(
-            src_ref=send_b.at[d], dst_ref=recv_b.at[d],
-            send_sem=sems.at[2, d], recv_sem=sems.at[3, d],
+            src_ref=send_b.at[h, d], dst_ref=recv_b.at[h, d],
+            send_sem=sems.at[h, 2, d], recv_sem=sems.at[h, 3, d],
             device_id=(z, chip_at(d) * 2 + core), device_id_type=MESH,
         )
 
-    def scatter_sum(acc, buffers):
+    def scatter_start(mine, buffers):
         send_a, recv_a, send_b, recv_b, sems = buffers
-        for d in list(range(1, chips)) + [0]:
-            q = chip_at(d)
-            send_a[q] = acc[q * 2 + (1 - core)].astype(BF16)
-            across_copy(buffers, q).start()
+        for h in range(send_a.shape[0]):
+            for d in list(range(1, chips)) + [0]:
+                q = chip_at(d)
+                send_a[h, q] = mine(h, q * 2 + (1 - core)).astype(BF16)
+                across_copy(buffers, h, q).start()
+        for h in range(send_a.shape[0]):
+            for d in range(1, chips):
+                q = chip_at(d)
+                across_copy(buffers, h, q).wait_recv()
+                send_b[h, d] = (mine(h, q * 2 + core) + recv_a[h, q].astype(F32)).astype(BF16)
+                between_copy(buffers, h, d).start()
+
+    def scatter_end(mine, buffers, h):
+        send_a, recv_a, send_b, recv_b, sems = buffers
+        across_copy(buffers, h, chip).wait_recv()
+        total = mine(h, me) + recv_a[h, chip].astype(F32)
         for d in range(1, chips):
-            q = chip_at(d)
-            across_copy(buffers, q).wait_recv()
-            send_b[d] = (acc[q * 2 + core] + recv_a[q].astype(F32)).astype(BF16)
-            between_copy(buffers, d).start()
-        across_copy(buffers, chip).wait_recv()
-        total = acc[me] + recv_a[chip].astype(F32)
-        for d in range(1, chips):
-            between_copy(buffers, d).wait_recv()
-            total = total + recv_b[d].astype(F32)
-        for d in range(chips):
-            across_copy(buffers, chip_at(d)).wait_send()
-        for d in range(1, chips):
-            between_copy(buffers, d).wait_send()
+            between_copy(buffers, h, d).wait_recv()
+            total = total + recv_b[h, d].astype(F32)
         return total
+
+    def scatter_sent(buffers):
+        for h in range(buffers[0].shape[0]):
+            for d in range(chips):
+                across_copy(buffers, h, chip_at(d)).wait_send()
+            for d in range(1, chips):
+                between_copy(buffers, h, d).wait_send()
 
     gather_start(0, dir_own, dir_all)
 
@@ -307,12 +315,22 @@
                 here = slice(b * fit_part, (b + 1) * fit_part)
                 fit_acc[b] += dot(k_buf[k, here, :], coef_low[...])
 
-    fitted = scatter_sum(fit_acc, fit_rs)
-    fit_own[...] = fitted.T.astype(BF16)
-    gather_start(1, fit_own, fit_all)
+    fit_pieces = fit_own.shape[0]
+    fit_piece = fit_part // fit_pieces
+
+    def fit_mine(h, block):
+        return fit_acc[block, h * fit_piece : (h + 1) * fit_piece, :]
+
+    scatter_start(fit_mine, fit_rs)
+    for h in range(fit_pieces):
+        fit_own[h] = scatter_end(fit_mine, fit_rs, h).T.astype(BF16)
+        gather_start(1 + h, fit_own.at[h], fit_all.at[h])
     img_acc[...] = jnp.zeros_like(img_acc)
-    gather_forward(1, fit_own, fit_all)
-    gather_end(1, fit_own, fit_all)
+    for h in range(fit_pieces):
+        gather_forward(1 + h, fit_own.at[h], fit_all.at[h])
+    for h in range(fit_pieces):
+        gather_end(1 + h, fit_own.at[h], fit_all.at[h])
+    scatter_sent(fit_rs)
 
     scale = float(rows_here * rows_n) ** -0.5
 
@@ -322,9 +340,9 @@
         def _():
             total = jnp.zeros((OUTS, CHUNK), F32)
             for b in range(cent_n):
-                total = total + dot(
-                    fit_all[b], k_buf[it, b * fit_part : (b + 1) * fit_part, :]
-                )
+                for h in range(fit_pieces):
+                    start = b * fit_part + h * fit_piece
+                    total = total + dot(fit_all[h, b], k_buf[it, start : start + fit_piece, :])
             grad[0][it] = total
 
         scan_step(grad, it)
@@ -337,7 +355,17 @@
             for b in range(cent_n):
                 img_acc[b] += dot(low, p_buf[k, :, b * part : (b + 1) * part])
 
-    image = scatter_sum(img_acc, img_rs).T + ridge_weight * dir_ref[...]
+    img_pieces = img_rs[0].shape[0]
+    img_piece = part // img_pieces
+
+    def img_mine(h, block):
+        return img_acc[block, :, h * img_piece : (h + 1) * img_piece]
+
+    scatter_start(img_mine, img_rs)
+    image = jnp.concatenate(
+        [scatter_end(img_mine, img_rs, h).T for h in range(img_pieces)], axis=0
+    )
+    image = image + ridge_weight * dir_ref[...]
     image_ref[...] = image
 
     def rows_sum(value):
@@ -390,6 +418,7 @@
     scan_sent(pick)
     scan_sent(coef)
     scan_sent(grad)
+    scatter_sent(img_rs)
 
 
 def update_kernel(sums_ref, image_ref, coef_ref, res_ref, dir_ref, coef_out, res_out, dir_out):
@@ -412,6 +441,8 @@
     chunks = centres_here // CHUNK
     chips = cent_n // 2
     fit_part = rows_here // cent_n
+    fit_pieces = 2 if fit_part % 256 == 0 else 1
+    img_pieces = 2 if part % 256 == 0 else 1
     vmem = pl.BlockSpec(memory_space=pltpu.VMEM)
 
     def scan(shape, own_dtype):
@@ -423,12 +454,12 @@
             pltpu.SemaphoreType.DMA((4, chunks)),
         )
 
-    def scatter(shape):
-        piece = (chips,) + shape
+    def scatter(pieces, shape):
+        piece = (pieces, chips) + shape
         return (
             pltpu.VMEM(piece, BF16), pltpu.VMEM(piece, BF16),
             pltpu.VMEM(piece, BF16), pltpu.VMEM(piece, BF16),
-            pltpu.SemaphoreType.DMA((4, chips)),
+            pltpu.SemaphoreType.DMA((pieces, 4, chips)),
         )
 
     image, sums = pl.pallas_call(
@@ -452,13 +483,13 @@
             pltpu.VMEM((CHUNK, OUTS), BF16),
             pltpu.VMEM((part, OUTS), BF16),
             pltpu.VMEM((cent_n, part, OUTS), BF16),
-            pltpu.VMEM((OUTS, fit_part), BF16),
-            pltpu.VMEM((cent_n, OUTS, fit_part), BF16),
-            pltpu.SemaphoreType.DMA((2, 4, chips)),
+            pltpu.VMEM((fit_pieces, OUTS, fit_part // fit_pieces), BF16),
+            pltpu.VMEM((fit_pieces, cent_n, OUTS, fit_part // fit_pieces), BF16),
+            pltpu.SemaphoreType.DMA((1 + fit_pieces, 4, chips)),
             pltpu.VMEM((cent_n, fit_part, OUTS), F32),
-            scatter((fit_part, OUTS)),
+            scatter(fit_pieces, (fit_part // fit_pieces, OUTS)),
             pltpu.VMEM((cent_n, OUTS, part), F32),
-            scatter((OUTS, part)),
+            scatter(img_pieces, (OUTS, part // img_pieces)),
             pltpu.VMEM((8, OUTS), F32),
             pltpu.VMEM((cent_n, 8, OUTS), F32),
             pltpu.VMEM((8, OUTS), F32),

time: 106 us -> 101 us (0.953)
  Pallas kernels: 106 us -> 101 us
    pallas_call x1, Pallas kernels: 103 us -> 98.3 us  [on_device(): pl.pallas_call(functools.partial(step_kernel, rows_n, cent_n), out_shape=...]
where the time goes in v3:
time: 101 us
  Pallas kernels  101 us (100%)
    pallas_call x1, Pallas kernels, on_device(): pl.pallas_call(functools.partial(step_kernel, rows_n, cent_n), out_shape=...  98.3 us
    pallas_call x1, Pallas kernels, on_device(): pl.pallas_call(update_kernel, out_shape=(piece, piece, piece), in_specs=[...  2.22 us

profile of v3, /device:TPU:0, one launch (start us, length us, event | category | flops | bytes accessed | tf_op | source)
XLA Modules:
  0.0 101.2 jit_solution(13078048184235383308)
XLA Ops:
  0.6 98.3 %falkon_step.1 = (f32[512,128]{1,0:T(8,128)}, f32[8,128]{1,0:T(8,128)}) custom-call(s32[8,1,256]{2,1,0:T(1,128)} %bitcast.3, f32[64,4096]{1,0:T(8,128)} %bitcast.2, bf16[2048,4096]{1,0:T(8,128)(2,1)} %p_hbm.1, f32[512,128]{1,0:T(8,128)} %res_ref.3, f32[512,128]{1,0:T(8,128)} %dir_ref.3), custom_call_target="tpu_custom_call" | custom-call | tf_op jit(solution)/shard_map/falkon_step/pallas_call | solution.py:465
  99.0 2.2 %falkon_update.1 = (f32[512,128]{1,0:T(8,128)}, f32[512,128]{1,0:T(8,128)}, f32[512,128]{1,0:T(8,128)}) custom-call(f32[8,128]{1,0:T(8,128)} %get-tuple-element.5.sums_ref, f32[512,128]{1,0:T(8,128)} %get-tuple-element.6.image_ref, f32[512,128]{1,0:T(8,128)} %coef_ref.1, f32[512,128]{1,0:T(8,128)} %res_ref.3, f32[512,128]{1,0:T(8,128)} %dir_ref.3), custom_call_target="tpu_custom_call" | custom-call | tf_op jit(solution)/shard_map/falkon_update/pallas_call | solution.py:506

commit v4 on v3

--- a/solution.py
+++ b/solution.py
@@ -11,7 +11,7 @@
 FEAT = 64
 OUTS = 128
 CHUNK = 256
-LAG = 3
+LAG = 4
 F32 = jnp.float32
 BF16 = jnp.bfloat16
 MESH = pl.DeviceIdType.MESH

time: 101 us -> 103 us (1.020)
    pallas_call x1, Pallas kernels: 98.3 us -> 99.8 us  [on_device(): pl.pallas_call(functools.partial(step_kernel, rows_n, cent_n), out_shape=...]
where the time goes in v4:
time: 103 us
  Pallas kernels  102 us (99%)
    pallas_call x1, Pallas kernels, on_device(): pl.pallas_call(functools.partial(step_kernel, rows_n, cent_n), out_shape=...  99.8 us
    pallas_call x1, Pallas kernels, on_device(): pl.pallas_call(update_kernel, out_shape=(piece, piece, piece), in_specs=[...  2.22 us

profile of v4, /device:TPU:0, one launch (start us, length us, event | category | flops | bytes accessed | tf_op | source)
XLA Modules:
  0.0 102.7 jit_solution(10280199241085507587)
XLA Ops:
  0.6 99.8 %falkon_step.1 = (f32[512,128]{1,0:T(8,128)}, f32[8,128]{1,0:T(8,128)}) custom-call(s32[8,1,256]{2,1,0:T(1,128)} %bitcast.3, f32[64,4096]{1,0:T(8,128)} %bitcast.2, bf16[2048,4096]{1,0:T(8,128)(2,1)} %p_hbm.1, f32[512,128]{1,0:T(8,128)} %res_ref.3, f32[512,128]{1,0:T(8,128)} %dir_ref.3), custom_call_target="tpu_custom_call" | custom-call | tf_op jit(solution)/shard_map/falkon_step/pallas_call | solution.py:465
  100.5 2.2 %falkon_update.1 = (f32[512,128]{1,0:T(8,128)}, f32[512,128]{1,0:T(8,128)}, f32[512,128]{1,0:T(8,128)}) custom-call(f32[8,128]{1,0:T(8,128)} %get-tuple-element.5.sums_ref, f32[512,128]{1,0:T(8,128)} %get-tuple-element.6.image_ref, f32[512,128]{1,0:T(8,128)} %coef_ref.1, f32[512,128]{1,0:T(8,128)} %res_ref.3, f32[512,128]{1,0:T(8,128)} %dir_ref.3), custom_call_target="tpu_custom_call" | custom-call | tf_op jit(solution)/shard_map/falkon_update/pallas_call | solution.py:506
